TPU v7x, 128 devices: a whole 4x4x4 slice. The times are simulated.
128 devices in a mesh: slab: 8 (over y, core), sub: 16 (over z, x).
Axes of the slice: x: 4, y: 4, z: 4, core: 2. Of those that a mesh axis runs over, the one named last changes fastest.
Arguments:
- positions: float32 [3, 8388608], P(None, ('slab', 'sub')), may hold values from 0 to 64, as said below
- masses: float32 [8388608], P(('slab', 'sub')), may hold values from 0.001 to 0.01
- leaf_counts: int32 [32768], P(('slab', 'sub')), may hold values from 64 to 256, as said below
- send_leaves: int32 [128, 256], P(('slab', 'sub')), may hold values from 0 to 255, as said below
- send_parents: int32 [128, 64], P(('slab', 'sub')), may hold values from 0 to 31, as said below
- near_pairs: int32 [128, 3, 256], P(('slab', 'sub')), may hold values from -1 to 511, as said below
- far_pairs: int32 [128, 3, 1024], P(('slab', 'sub')), may hold values from -1 to 511, as said below
- parent_pairs: int32 [128, 3, 64], P(('slab', 'sub')), may hold values from -1 to 95, as said below
Outputs:
- field: float32 [4, 8388608], P(None, ('slab', 'sub'))
Inputs may be any that keep to these rules, and one draw needn't show every extreme that they name: `positions`: the coordinates of a body of leaf c on device (s, u) lie within one unit above that leaf's integer coordinates along each dimension. `leaf_counts`: every device has a leaf whose 256 slots are all used. `send_leaves`: within one direction of a row, the 64 leaves are different. `send_parents`: within one direction of a row, the 16 parent cells are different. `near_pairs`: row 0 is an own leaf, row 1 a leaf table entry or -1 for an unused entry (unused entries come last), row 2 the z image -1, 0 or 1 (0 where unused). Own pairs have a < b; no pair repeats; pairs are leaves at most one leaf apart along each dimension after the image. `far_pairs`: as near_pairs, for leaves whose squared separation after the image is 4 to 12 leaf units. `parent_pairs`: as near_pairs, for parent cells whose squared separation after the image is 2 parent units or more, with the parent table.
All inputs are finite; a program needn't handle non-finite values.
Results may differ from a plain program's by a relative error of at most 0.0003.
Values sent between devices are 32-bit elements; how exact they have to be, the bound alone decides.
A program may use at most 320 MiB of HBM per device.

v0:
```python
import functools

import jax
import jax.numpy as jnp
from jax import lax
from jax.experimental import pallas as pl
from jax.experimental.pallas import tpu as pltpu
from jax.sharding import PartitionSpec as P

CX = 2
CY = 4
CZ = 32
LEAVES = 256
LEAF = 256
PARENTS = 32
SLOTS = 64
PSLOTS = 16
NEAR = 256
FAR = 1024
PFAR = 64
PAY = SLOTS + 5
SOFT = 0.0025
WIDTH = 8
SELF_WIDTH = 16
CLASSES = (128, 192, 256)
SORTED = 384
slab_steps = (1, 0, 1, 1)
sub_steps = (0, 1, 1, -1)
f32 = jnp.float32
bf16 = jnp.bfloat16

ALPHAS = [
    (i, j, d - i - j) for d in range(5) for i in range(d, -1, -1) for j in range(d - i, -1, -1)
]
AT = {a: n for n, a in enumerate(ALPHAS)}
FACT = (1.0, 1.0, 2.0, 6.0, 24.0)
TABLE = LEAVES + 4 * 128 + 128


def afact(alpha):
    return FACT[alpha[0]] * FACT[alpha[1]] * FACT[alpha[2]]


def add(a, b):
    return (a[0] + b[0], a[1] + b[1], a[2] + b[2])


def unit(axis):
    return tuple(1 if k == axis else 0 for k in range(3))


def split3(value):
    one = value.astype(bf16)
    rest = value - one.astype(f32)
    two = rest.astype(bf16)
    three = (rest - two.astype(f32)).astype(bf16)
    return one, two, three


def dot_nn(a, b):
    return lax.dot_general(a, b, (((1,), (0,)), ((), ())), preferred_element_type=f32)


def dot_nt(a, b):
    return lax.dot_general(a, b, (((1,), (1,)), ((), ())), preferred_element_type=f32)


def dot_tn(a, b):
    return lax.dot_general(a, b, (((0,), (0,)), ((), ())), preferred_element_type=f32)


def pick(values, onehot, transposed=False):
    parts = jnp.concatenate([part.astype(f32) for part in split3(values)], 0).astype(bf16)
    out = dot_nt(parts, onehot) if transposed else dot_nn(parts, onehot)
    rows = values.shape[0]
    return out[:rows] + out[rows : 2 * rows] + out[2 * rows :]


def iota(shape, dim):
    return lax.broadcasted_iota(jnp.int32, shape, dim)


def onehot_rows(count, ids):
    hit = iota((count, ids.shape[1]), 0) == ids
    return jnp.where(hit, 1.0, 0.0).astype(bf16)


def id_row(sent_leaves, sent_parents, q):
    return jnp.concatenate(
        [
            sent_leaves[:, q * SLOTS : (q + 1) * SLOTS],
            sent_parents[:, q * PSLOTS : (q + 1) * PSLOTS],
            jnp.full((1, 128 - SLOTS - PSLOTS), -1, jnp.int32),
        ],
        1,
    )


def put_slab(slab_ref, c, slab):
    wide = jnp.concatenate([slab, jnp.zeros((4, LEAF), f32)], 0)
    for half in range(2):
        rows = pl.ds(pl.multiple_of(half * LEAVES * 8 + c * 8, 8), 8)
        slab_ref[rows, :] = wide[:, half * 128 : half * 128 + 128]


def get_rows(slab_ref, comp):
    return jnp.concatenate(
        [slab_ref[pl.ds(half * LEAVES * 8 + comp, LEAVES, stride=8), :] for half in range(2)], 1
    )


def monomials(x, y, z, w):
    made = {(0, 0, 0): w}
    for alpha in ALPHAS[1:]:
        for axis, value in ((2, z), (1, y), (0, x)):
            if alpha[axis]:
                lower = tuple(alpha[k] - (k == axis) for k in range(3))
                made[alpha] = made[lower] * value
                break
    return made


def shift_moments(moments, offsets):
    choose = ((1,), (1, 1), (1, 2, 1), (1, 3, 3, 1), (1, 4, 6, 4, 1))
    for axis in range(3):
        powers = [None, offsets[axis]]
        for _ in range(3):
            powers.append(powers[-1] * offsets[axis])
        moved = {}
        for alpha in ALPHAS:
            total = moments[alpha]
            for k in range(alpha[axis]):
                lower = tuple(k if q == axis else alpha[q] for q in range(3))
                total = total + moments[lower] * powers[alpha[axis] - k] * float(
                    choose[alpha[axis]][k]
                )
            moved[alpha] = total
        moments = moved
    return moments


def leaf_lanes():
    lane = iota((1, LEAVES), 1)
    return lane // (CY * CZ), lane // CZ % CY, lane % CZ


def parent_offsets():
    cell_x, cell_y, cell_z = leaf_lanes()
    return [(cell % 2).astype(f32) - 0.5 for cell in (cell_x, cell_y, cell_z)]


def front_kernel(
    at_ref, counts_hbm, row_hbm, send_hbm, parents_hbm, pos_hbm, mass_hbm,
    own_ref, cells_ref, pcells_ref, pay0, pay1, pay2, pay3, turned_ref, ordered_ref,
    slab_ref, pos_ref, mass_ref, counts_ref, send_ref, counts_row, sent_leaves, sent_parents, sem,
):
    pays = (pay0, pay1, pay2, pay3)
    pieces = CX * CY
    bodies = LEAVES * LEAF // pieces
    places = [
        pltpu.make_async_copy(
            pos_hbm.at[:, pl.ds(n * bodies, bodies)], pos_ref.at[:, pl.ds(n * bodies, bodies)],
            sem.at[6 + n],
        )
        for n in range(pieces)
    ]
    smaller = [
        pltpu.make_async_copy(source, target, sem.at[n])
        for n, (source, target) in enumerate(
            (
                (counts_hbm, counts_ref), (mass_hbm, mass_ref), (send_hbm, send_ref),
                (row_hbm, counts_row), (send_hbm, sent_leaves), (parents_hbm, sent_parents),
            )
        )
    ]
    for copy in smaller[:2] + places + smaller[2:]:
        copy.start()
    for copy in smaller:
        copy.wait()
    base_x = at_ref[0] * CX
    base_y = at_ref[1] * CY
    row4 = iota((4, LEAF), 0)
    lane = iota((1, LEAF), 1)
    batch = 8

    for x in range(CX):
        for y in range(CY):
            centre = jnp.where(row4 == 1, (base_x + x).astype(f32) + 0.5, 0.0)
            centre = jnp.where(row4 == 2, (base_y + y).astype(f32) + 0.5, centre)
            places[x * CY + y].wait()

            def some_leaves(step, _, x=x, y=y, centre=centre):
                low = step * batch
                first = (x * CY + y) * CZ + low
                from_z = jnp.where(row4 == 3, low.astype(f32) + 0.5, centre)
                for k in range(batch):
                    c = first + k
                    start = pl.multiple_of(c * LEAF, LEAF)
                    place = pos_ref[:, pl.ds(start, LEAF)]
                    mass = jnp.concatenate(
                        [mass_ref[pl.ds(2 * c, 1), :], mass_ref[pl.ds(2 * c + 1, 1), :]], 1
                    )
                    weight = jnp.where(lane < counts_ref[c], mass, 0.0)
                    slab = jnp.concatenate([weight, place], 0) - (
                        from_z + jnp.where(row4 == 3, float(k), 0.0)
                    )
                    own_ref[c] = slab
                    put_slab(slab_ref, c, slab)
                return 0

            lax.fori_loop(0, CZ // batch, some_leaves, 0)

    for comp in range(4):
        turned_ref[comp] = get_rows(slab_ref, comp).T

    for half in range(2):
        lanes = slice(half * 128, half * 128 + 128)

        def chunk(step, totals):
            rows = pl.ds(pl.multiple_of(step * 8, 8), 8)
            w, x, y, z = [turned_ref[comp, rows, lanes] for comp in range(4)]
            made = monomials(x, y, z, w)
            return tuple(total + made[alpha] for total, alpha in zip(totals, ALPHAS))

        totals = lax.fori_loop(
            0, LEAF // 8, chunk, tuple(jnp.zeros((8, 128), f32) for _ in ALPHAS), unroll=2
        )
        for n, total in enumerate(totals):
            cells_ref[n : n + 1, lanes] = jnp.sum(total, 0, keepdims=True)

    cell_x, cell_y, cell_z = leaf_lanes()
    cells_ref[35:36, :] = (base_x + cell_x).astype(f32) + 0.5
    cells_ref[36:37, :] = (base_y + cell_y).astype(f32) + 0.5
    cells_ref[37:38, :] = cell_z.astype(f32) + 0.5
    cells_ref[38:39, :] = counts_row[...].astype(f32)
    cells_ref[39:40, :] = jnp.zeros((1, LEAVES), f32)

    moments = {alpha: cells_ref[n : n + 1, :] for n, alpha in enumerate(ALPHAS)}
    moved = shift_moments(moments, parent_offsets())
    moved = jnp.concatenate(
        [moved[alpha] for alpha in ALPHAS] + [jnp.zeros((5, LEAVES), f32)], 0
    )
    parent_of = (iota((LEAVES, 128), 0) // CZ % CY // 2) * (CZ // 2) + iota(
        (LEAVES, 128), 0
    ) % CZ // 2
    belongs = jnp.where(parent_of == iota((LEAVES, 128), 1), 1.0, 0.0).astype(bf16)
    pcells = pick(moved, belongs)
    plane = iota((40, 128), 1)
    prow = iota((40, 128), 0)
    pcells = jnp.where(prow == 35, (base_x + 1).astype(f32), pcells)
    pcells = jnp.where(
        prow == 36, (base_y + 2 * (plane // (CZ // 2))).astype(f32) + 1.0, pcells
    )
    pcells = jnp.where(prow == 37, (2 * (plane % (CZ // 2))).astype(f32) + 1.0, pcells)
    pcells_ref[...] = pcells

    lane128 = iota((1, 128), 1)
    for q in range(4):
        pay = pays[q]

        def copy_leaf(k, _, pay=pay, q=q):
            pay[k] = own_ref[send_ref[0, q * SLOTS + k]]
            return 0

        lax.fori_loop(0, SLOTS, copy_leaf, 0, unroll=8)
        ids = id_row(sent_leaves, sent_parents, q)
        leaf_hot = onehot_rows(LEAVES, jnp.where(lane128 < SLOTS, ids, -1))
        parent_hot = onehot_rows(128, jnp.where(lane128 >= SLOTS, ids, -1))
        block = pick(cells_ref[...], leaf_hot) + pick(pcells, parent_hot)
        put_block(pay, block)

    counts = counts_row[...]
    group = jnp.where(counts <= 128, 0, jnp.where(counts <= 192, 1, 2))
    sort_lists(iota((1, LEAVES), 1).astype(f32) + 1.0, group, SELF_WIDTH, ordered_ref)


def put_block(pay, block):
    for s in range(5):
        pay[SLOTS + s, :, 0:128] = block[4 * s : 4 * s + 4]
        pay[SLOTS + s, :, 128:256] = block[20 + 4 * s : 24 + 4 * s]


def get_block(tail):
    return jnp.concatenate(
        [tail(s)[:, 0:128] for s in range(5)] + [tail(s)[:, 128:256] for s in range(5)], 0
    )


VM = pl.BlockSpec(memory_space=pltpu.VMEM)
SM = pl.BlockSpec(memory_space=pltpu.SMEM)
HB = pl.BlockSpec(memory_space=pl.ANY)
HBM = pl.BlockSpec(memory_space=pltpu.MemorySpace.HBM)
PARAMS = dict(vmem_limit_bytes=24 * 1024 * 1024)


def in_hbm(value):
    return pltpu.with_memory_space_constraint(value, pltpu.MemorySpace.HBM)


def shaped(*shape):
    return jax.ShapeDtypeStruct(shape, f32)


def front(at, counts, send_leaves, send_parents, positions, masses):
    return pl.pallas_call(
        front_kernel,
        name="front",
        out_shape=[
            shaped(LEAVES, 4, LEAF), shaped(40, LEAVES), shaped(40, 128),
        ] + [shaped(PAY, 4, LEAF)] * 4 + [
            shaped(4, LEAF, LEAVES), jax.ShapeDtypeStruct((2, SORTED), jnp.int32),
        ],
        in_specs=[SM] + [HBM] * 6,
        out_specs=[VM] * 9,
        scratch_shapes=[
            pltpu.VMEM((LEAVES * 16, 128), f32),
            pltpu.VMEM((3, LEAVES * LEAF), f32),
            pltpu.VMEM((LEAVES * 2, 128), f32),
            pltpu.SMEM((LEAVES,), jnp.int32),
            pltpu.SMEM((1, 4 * SLOTS), jnp.int32),
            pltpu.VMEM((1, LEAVES), jnp.int32),
            pltpu.VMEM((1, 4 * SLOTS), jnp.int32),
            pltpu.VMEM((1, 4 * PSLOTS), jnp.int32),
            pltpu.SemaphoreType.DMA((6 + CX * CY,)),
        ],
        compiler_params=pltpu.CompilerParams(**PARAMS),
    )(
        at,
        *map(
            in_hbm,
            (
                counts, counts.reshape(1, LEAVES), send_leaves, send_parents, positions,
                masses.reshape(-1, 128),
            ),
        ),
    )


def slab8(slab):
    return jnp.concatenate([slab, jnp.zeros((4, LEAF), f32)], 0)


def b_form(points):
    row = iota(points.shape, 0)
    square = jnp.sum(jnp.where(row == 0, 0.0, points * points), 0, keepdims=True)
    return jnp.where(row == 4, square, points)


def a_form(formed):
    row = iota(formed.shape, 0)
    value = jnp.where(row == 0, formed[4:5] + SOFT, -2.0 * formed)
    return jnp.where(row == 4, 1.0, value)


def widen(value):
    one = value.astype(bf16).astype(f32)
    rest = value - one
    two = rest.astype(bf16).astype(f32)
    return one, two, rest - two


def squares(a_formed, b_formed):
    a1, a2, a3 = widen(a_form(a_formed))
    b1, b2, b3 = widen(b_formed)
    left = jnp.concatenate([a1, a1, a2, a2, a1, a3], 0).astype(bf16)
    right = jnp.concatenate([b1, b2, b1, b2, b3, b1], 0).astype(bf16)
    return dot_tn(left, right)


def weighted(formed, weight):
    parts = widen(formed * weight)
    return jnp.concatenate(parts + (jnp.zeros_like(parts[0]),), 0).astype(bf16)


def sources(points, weight):
    return weighted(b_form(points), weight)


def fold(out):
    total = out[0:8]
    for first in range(8, out.shape[0] // 8 * 8, 8):
        total = total + out[first : first + 8]
    return total


def finish(total, points):
    row = iota(points.shape, 0)
    field = total - points * total[0:1]
    sign = jnp.where(row == 0, -SOFT, jnp.where(row == 4, -1.0, 1.0))
    terms = jnp.where(row == 4, total, points * (field + total)) * sign
    return jnp.where(row == 0, jnp.sum(terms, 0, keepdims=True), field)[0:4]


def load_points(slab):
    wide = slab8(slab)
    row = iota((8, LEAF), 0)
    return jnp.where(row == 0, 1.0, wide), slab[0:1]


def self_kernel(part, list_ref, own_ref, *refs):
    out_ref = refs[-1]
    before_ref = refs[0]
    if not part:

        def begin(c, _):
            out_ref[c] = jnp.zeros((8, LEAF), f32)
            return 0

        lax.fori_loop(0, LEAVES, begin, 0, unroll=8)

    def place_of(step, k):
        code = list_ref[0, step * SELF_WIDTH + k]
        leaf = jnp.maximum(code - 1, 0)
        return leaf, jnp.where(code > 0, leaf, LEAVES)

    def some_leaves(step, rows, lanes):
        places = [place_of(step, k) for k in range(SELF_WIDTH)]
        loaded = []
        for leaf, _ in places:
            points, weight = load_points(own_ref[leaf])
            right = points[:, :lanes]
            formed = b_form(right)
            loaded.append((formed[:, :rows], weight[:, :rows], right, formed))
        spaced = [squares(left, formed) for left, _, _, formed in loaded]
        apart = jnp.where(iota((rows, lanes), 0) == iota((rows, lanes), 1), 0.0, 1.0)
        cubes = []
        for value in spaced:
            inverse = lax.rsqrt(value) * apart
            cubes.append(inverse * inverse * inverse)
        high = [cube.astype(bf16) for cube in cubes]
        done = []
        for cube, top, (left, weight, right, _), (leaf, _) in zip(cubes, high, loaded, places):
            low = (cube - top.astype(f32)).astype(bf16)
            side = weighted(left, weight)
            value = fold(dot_nn(side, top)) + fold(dot_nn(side[0:16], low))
            if part:
                value = finish(value + before_ref[leaf, :, 0:lanes], right)
            done.append(value)
        for (_, place), value in zip(places, done):
            out_ref[place, :, 0:lanes] = value

    def finish_some(step):
        places = [place_of(step, k) for k in range(SELF_WIDTH)]
        done = [finish(before_ref[leaf], load_points(own_ref[leaf])[0]) for leaf, _ in places]
        for (_, place), value in zip(places, done):
            out_ref[place] = value

    for n, rows in enumerate(CLASSES):
        first = list_ref[1, n]
        end = list_ref[1, n + 1]
        middle = (first + end + n % 2) >> 1
        lanes = 128 if rows == 128 else LEAF

        def body(step, _, rows=rows, lanes=lanes):
            some_leaves(step, rows, lanes)
            return 0

        lax.fori_loop(middle if part else first, end if part else middle, body, 0)
        if part:

            def rest(step, _):
                finish_some(step)
                return 0

            lax.fori_loop(first, middle, rest, 0)


def self_part(part, ordered, own, *before):
    return pl.pallas_call(
        functools.partial(self_kernel, part),
        name="self_part",
        out_shape=shaped(LEAVES + 8, 4 if part else 8, LEAF),
        in_specs=[SM, VM] + [VM] * part,
        out_specs=VM,
        cost_estimate=pl.CostEstimate(
            flops=LEAVES * 20_000_000, bytes_accessed=LEAVES * 8192, transcendentals=0
        ),
        compiler_params=pltpu.CompilerParams(**PARAMS),
    )(ordered, own, *before)


def near_kernel(
    list_ref, own_ref, in0, in1, in2, in3, backs_ref, self_ref,
    out_ref, pay0, pay1, pay2, pay3, table, total, shifts, formed_r, kept_c, sem, *held,
):
    pays = (pay0, pay1, pay2, pay3)
    copies = [
        pltpu.make_async_copy(own_ref, table.at[pl.ds(0, LEAVES)], sem.at[0]),
        pltpu.make_async_copy(self_ref.at[pl.ds(0, LEAVES)], total.at[pl.ds(0, LEAVES)], sem.at[5]),
    ]
    for q, part in enumerate((in0, in1, in2, in3)):
        copies.append(
            pltpu.make_async_copy(
                part.at[pl.ds(0, SLOTS)],
                table.at[pl.ds(LEAVES + q * SLOTS, SLOTS)],
                sem.at[1 + q],
            )
        )
    for copy in copies:
        copy.start()

    def clear(c, _):
        total[c] = jnp.zeros((8, LEAF), f32)
        return 0

    lax.fori_loop(LEAVES, 2 * LEAVES + 8, clear, 0, unroll=8)
    row = iota((8, 128), 0)
    for code in range(27):
        step = (code % 3 - 1, code // 3 % 3 - 1, code // 9 - 1)
        value = jnp.zeros((8, 128), f32)
        for k in range(3):
            value = jnp.where(row == k + 1, float(step[k]), value)
        shifts[code] = value
    for copy in copies:
        copy.wait()

    def decode(group, k):
        code = list_ref[0, group * WIDTH + k]
        value = jnp.maximum(code - 1, 0)
        return value & 511, (value >> 9) & 511, value >> 18, code > 0

    def shift_of(code):
        half = shifts[code]
        return jnp.concatenate([half, half], 1)

    def spaced(group, k, rows):
        r, c, code, _ = decode(group, k)
        points_r, _ = load_points(table[r])
        points_c, _ = load_points(table[c])
        points_r = (points_r + shift_of(code))[:, :rows]
        formed = b_form(points_r)
        formed_r[k, :, 0:rows] = formed
        kept_c[k] = points_c
        return squares(formed, b_form(points_c))

    def keep(k, rows, value):
        inverse = lax.rsqrt(value)
        held[k][0:rows, :] = (inverse * inverse * inverse).astype(bf16)

    def products(group, k, rows):
        r, c, code, live = decode(group, k)
        cube = held[k][0:rows, :]
        side_r = weighted(formed_r[k, :, 0:rows], table[r, 0:1, 0:rows])
        to_c = fold(dot_nn(side_r, cube))
        side_c = sources(kept_c[k] - shift_of(code), table[c, 0:1, :])
        to_r = fold(dot_nt(side_c, cube))
        return jnp.where(live, r, 2 * LEAVES), jnp.where(live, c, 2 * LEAVES), to_r, to_c

    def settle(done, rows):
        for r, c, to_r, to_c in done:
            total[r, :, 0:rows] = total[r, :, 0:rows] + to_r
            total[c] = total[c] + to_c

    for n, rows in enumerate(CLASSES):
        first = list_ref[1, n]
        end = list_ref[1, n + 1]

        @pl.when(end > first)
        def _(first=first, end=end, rows=rows):
            for k in range(WIDTH):
                keep(k, rows, spaced(first, k, rows))

            def advance(group, _):
                done = []
                for k in range(WIDTH):
                    done.append(products(group, k, rows))
                    keep(k, rows, spaced(group + 1, k, rows))
                settle(done, rows)
                return 0

            lax.fori_loop(first, end - 1, advance, 0)
            settle([products(end - 1, k, rows) for k in range(WIDTH)], rows)

    store = pltpu.make_async_copy(total.at[pl.ds(0, LEAVES)], out_ref, sem.at[6])
    store.start()
    for q in range(4):

        def finish_other(k, _, q=q):
            points, _ = load_points(table[LEAVES + q * SLOTS + k])
            pays[q][k] = finish(total[LEAVES + q * SLOTS + k], points)
            return 0

        lax.fori_loop(0, SLOTS, finish_other, 0, unroll=8)
        put_block(pays[q], backs_ref[q])
    store.wait()


def near_part(ordered, own, incoming, backs, self0):
    return pl.pallas_call(
        near_kernel,
        name="near_part",
        out_shape=[shaped(LEAVES, 8, LEAF)] + [shaped(PAY, 4, LEAF)] * 4,
        in_specs=[SM, HB, HB, HB, HB, HB, VM, HB],
        out_specs=[HB] + [VM] * 4,
        scratch_shapes=[
            pltpu.VMEM((2 * LEAVES, 4, LEAF), f32),
            pltpu.VMEM((2 * LEAVES + 8, 8, LEAF), f32),
            pltpu.VMEM((27, 8, 128), f32),
            pltpu.VMEM((WIDTH, 8, LEAF), f32),
            pltpu.VMEM((WIDTH, 8, LEAF), f32),
            pltpu.SemaphoreType.DMA((7,)),
        ] + [pltpu.VMEM((LEAF, LEAF), bf16)] * WIDTH,
        cost_estimate=pl.CostEstimate(
            flops=NEAR * 80_000_000, bytes_accessed=4_000_000, transcendentals=0
        ),
        compiler_params=pltpu.CompilerParams(**PARAMS),
    )(ordered, own, *incoming, backs, self0)


def sort_lists(code, group, width, out_ref):
    count = code.shape[1]
    hot = jnp.where(iota((8, count), 0) == group, 1.0, 0.0)
    earlier = jnp.where(iota((count, count), 0) < iota((count, count), 1), 1.0, 0.0).astype(bf16)
    before = dot_nn(hot.astype(bf16), earlier)
    members = jnp.sum(hot, 1, keepdims=True)
    lane = iota((1, SORTED), 1)
    place = jnp.zeros((1, count), f32)
    groups = jnp.zeros((1, 1), f32)
    ends = jnp.zeros((1, SORTED), f32)
    for n in range(len(CLASSES)):
        place = place + hot[n : n + 1] * (before[n : n + 1] + groups * width)
        groups = groups + jnp.floor((members[n : n + 1] + (width - 1)) * (1.0 / width))
        ends = jnp.where(lane == n + 1, groups, ends)
    place = jnp.where(group >= 0, place, -1.0).astype(jnp.int32)
    ordered = pick(jnp.broadcast_to(code, (8, count)), onehot_rows(SORTED, place), True)
    out_ref[0:1, :] = ordered[0:1].astype(jnp.int32)
    out_ref[1:2, :] = ends.astype(jnp.int32)


def derivatives(x, y, z):
    square = x * x + y * y + z * z
    inverse = 1.0 / jnp.sqrt(square)
    inverse2 = inverse * inverse
    table = {(0, (0, 0, 0)): inverse}
    for m in range(1, 5):
        table[(m, (0, 0, 0))] = table[(m - 1, (0, 0, 0))] * inverse2 * float(-(2 * m - 1))
    place = (x, y, z)

    def entry(m, alpha):
        key = (m, alpha)
        if key not in table:
            axis = [k for k in range(3) if alpha[k]][0]
            lower = tuple(alpha[k] - (k == axis) for k in range(3))
            value = place[axis] * entry(m + 1, lower)
            if lower[axis]:
                lowest = tuple(lower[k] - (k == axis) for k in range(3))
                value = value + float(lower[axis]) * entry(m + 1, lowest)
            table[key] = value
        return table[key]

    return {alpha: entry(0, alpha) for alpha in ALPHAS}


def mutual(a_ref, b_ref, to_a, to_b):
    def rows(n):
        return pl.ds(n * 8, 8)

    lift = a_ref[rows(38), :]
    live = a_ref[rows(39), :] > 0.5
    gap = [
        jnp.where(live, a_ref[rows(35 + k), :] - b_ref[rows(35 + k), :] - (lift if k == 2 else 0.0), 3.0)
        for k in range(3)
    ]
    made = derivatives(*gap)
    for beta in ALPHAS:
        sum_a = None
        sum_b = None
        for alpha in ALPHAS:
            if sum(alpha) + sum(beta) > 4:
                continue
            tensor = made[add(alpha, beta)]
            scale = 1.0 / afact(alpha)
            sign_a = -((-1.0) ** sum(alpha)) * scale
            sign_b = -((-1.0) ** sum(beta)) * scale
            term_a = b_ref[rows(AT[alpha]), :] * sign_a * tensor
            term_b = a_ref[rows(AT[alpha]), :] * sign_b * tensor
            sum_a = term_a if sum_a is None else sum_a + term_a
            sum_b = term_b if sum_b is None else sum_b + term_b
        to_a[rows(AT[beta]), :] = jnp.where(live, sum_a, 0.0)
        to_b[rows(AT[beta]), :] = jnp.where(live, sum_b, 0.0)


def far_kernel(
    image_ref, far_ref, parent_ref, near_ref, cells_ref, pcells_ref, in0, in1, in2, in3,
    leaf_ref, par_ref, backs_ref, ordered_ref, tails, table, left, right, to_a, to_b, total, sem,
):
    copies = []
    for q, part in enumerate((in0, in1, in2, in3)):
        copies.append(
            pltpu.make_async_copy(part.at[pl.ds(SLOTS, 5)], tails.at[q], sem.at[q])
        )
    for copy in copies:
        copy.start()
    table[:, 0:LEAVES] = cells_ref[...]
    table[:, LEAVES + 512 :] = pcells_ref[...]
    row = iota((40, 128), 0)
    to_a[...] = jnp.zeros_like(to_a)
    to_b[...] = jnp.zeros_like(to_b)
    left[...] = jnp.zeros_like(left)
    right[...] = jnp.zeros_like(right)
    for copy in copies:
        copy.wait()
    for q in range(4):
        block = get_block(lambda s, q=q: tails[q, s])
        block = block + jnp.where(
            row == 35, image_ref[q, 0], jnp.where(row == 36, image_ref[q, 1], 0.0)
        )
        table[:, LEAVES + q * 128 : LEAVES + q * 128 + 128] = block
    parts = jnp.concatenate([part.astype(f32) for part in split3(table[...])], 0).astype(bf16)
    total[...] = jnp.zeros_like(total)

    def gathered(hot, first, count):
        out = dot_nn(parts[:, first : first + count], hot)
        return out[0:40] + out[40:80] + out[80:120]

    def leaf_entry(ids):
        other = ids - LEAVES
        return jnp.where(ids < LEAVES, ids, LEAVES + other // SLOTS * 128 + other % SLOTS)

    def parent_entry(ids):
        other = ids - PARENTS
        return jnp.where(
            ids < PARENTS, LEAVES + 512 + ids, LEAVES + other // PSLOTS * 128 + SLOTS + other % PSLOTS
        )

    def hots(ids_a, ids_b, parents):
        if parents:
            return (
                onehot_rows(128, ids_a), LEAVES + 512, 128,
                onehot_rows(640, parent_entry(ids_b) - LEAVES), LEAVES, 640,
            )
        return (
            onehot_rows(LEAVES, ids_a), 0, LEAVES,
            onehot_rows(768, leaf_entry(ids_b)), 0, 768,
        )

    def load(ids_a, ids_b, lifts, g, parents):
        hot_a, first_a, count_a, hot_b, first_b, count_b = hots(ids_a, ids_b, parents)
        from_a = gathered(hot_a, first_a, count_a)
        from_b = gathered(hot_b, first_b, count_b)
        live = jnp.where(ids_b >= 0, 1.0, 0.0)
        from_a = jnp.where(row == 38, lifts.astype(f32) * float(CZ), from_a)
        from_a = jnp.where(row == 39, live, from_a)
        left[pl.ds(g, 40, stride=8), :] = from_a
        right[pl.ds(g, 40, stride=8), :] = from_b

    def store(ids_a, ids_b, g, parents):
        hot_a, first_a, count_a, hot_b, first_b, count_b = hots(ids_a, ids_b, parents)
        sum_a = pick(to_a[pl.ds(g, 40, stride=8), :], hot_a, True)
        sum_b = pick(to_b[pl.ds(g, 40, stride=8), :], hot_b, True)
        total[:, first_a : first_a + count_a] += sum_a
        total[:, first_b : first_b + count_b] += sum_b

    for g in range(FAR // 128):
        lanes = slice(g * 128, g * 128 + 128)
        load(far_ref[0, :, lanes], far_ref[1, :, lanes], far_ref[2, :, lanes], g, False)
    mutual(left, right, to_a, to_b)
    for g in range(FAR // 128):
        lanes = slice(g * 128, g * 128 + 128)
        store(far_ref[0, :, lanes], far_ref[1, :, lanes], g, False)
    ids_a, ids_b, lifts = [
        jnp.concatenate([parent_ref[k], jnp.full((1, 128 - PFAR), -(k == 1), jnp.int32)], 1)
        for k in range(3)
    ]
    load(ids_a, ids_b, lifts, 0, True)
    mutual(left, right, to_a, to_b)
    store(ids_a, ids_b, 0, True)

    ids_a, ids_b, lifts = near_ref[0], near_ref[1], near_ref[2]
    hot_a, _, _, hot_b, _, _ = hots(ids_a, ids_b, False)
    from_a = gathered(hot_a, 0, LEAVES)[35:39]
    from_b = gathered(hot_b, 0, 768)[35:39]
    count_a, count_b = from_a[3:4], from_b[3:4]
    fewer = jnp.minimum(count_a, count_b)
    swap = count_b < count_a
    group = jnp.where(fewer <= 128.0, 0, jnp.where(fewer <= 192.0, 1, 2))
    group = jnp.where(ids_b >= 0, group, -1)
    moved = jnp.zeros((1, NEAR), f32)
    for k in range(3):
        apart = from_a[k : k + 1] - from_b[k : k + 1]
        if k == 2:
            apart = apart - lifts.astype(f32) * float(CZ)
        apart = jnp.where(swap, -apart, apart)
        moved = moved + (apart + 1.0) * float(3**k)
    rows = jnp.where(swap, ids_b, ids_a)
    columns = jnp.where(swap, ids_a, ids_b)
    code = 1.0 + rows.astype(f32) + columns.astype(f32) * 512.0 + moved * 262144.0
    sort_lists(jnp.where(ids_b >= 0, code, 0.0), group, WIDTH, ordered_ref)

    leaf_ref[...] = total[:, 0:LEAVES]
    par_ref[...] = total[:, LEAVES + 512 :]
    for q in range(4):
        backs_ref[q] = total[:, LEAVES + q * 128 : LEAVES + q * 128 + 128]


def far_part(image, far, parent, near, cells, pcells, incoming):
    return pl.pallas_call(
        far_kernel,
        name="far_part",
        out_shape=[
            shaped(40, LEAVES), shaped(40, 128), shaped(4, 40, 128),
            jax.ShapeDtypeStruct((2, SORTED), jnp.int32),
        ],
        in_specs=[SM, VM, VM, VM, VM, VM, HB, HB, HB, HB],
        out_specs=[VM] * 4,
        scratch_shapes=[
            pltpu.VMEM((4, 5, 4, LEAF), f32),
            pltpu.VMEM((40, TABLE), f32),
        ] + [pltpu.VMEM((320, 128), f32)] * 4 + [
            pltpu.VMEM((40, TABLE), f32),
            pltpu.SemaphoreType.DMA((4,)),
        ],
        compiler_params=pltpu.CompilerParams(**PARAMS),
    )(
        image, far.transpose(1, 0, 2), parent.transpose(1, 0, 2), near.transpose(1, 0, 2),
        cells, pcells, *incoming,
    )


def shift_terms(terms, offsets):
    for axis in range(3):
        powers = [None, offsets[axis]]
        for _ in range(3):
            powers.append(powers[-1] * offsets[axis])
        moved = {}
        for alpha in ALPHAS:
            total = terms[alpha]
            for k in range(1, 5 - sum(alpha)):
                upper = tuple(alpha[q] + k * (q == axis) for q in range(3))
                total = total + terms[upper] * powers[k] * (1.0 / FACT[k])
            moved[alpha] = total
        terms = moved
    return terms


def horner(coefs, x):
    value = coefs[-1]
    for coef in reversed(coefs[:-1]):
        value = value * x + coef
    return value


def horner_both(coefs, x):
    value, slope = coefs[-1], None
    for coef in reversed(coefs[:-1]):
        slope = value if slope is None else slope * x + value
        value = value * x + coef
    return value, slope


def polynomial(get, x, y, z):
    over_y, over_dy, over_dz = [], [], []
    for i in range(5):
        over_z = [
            horner_both([get((i, j, k)) for k in range(5 - i - j)], z) for j in range(5 - i)
        ]
        value, slope = horner_both([pair[0] for pair in over_z], y)
        over_y.append(value)
        if i < 4:
            over_dy.append(slope)
            over_dz.append(horner([pair[1] for pair in over_z[:-1]], y))
    value, slope = horner_both(over_y, x)
    return value, slope, horner(over_dy, x), horner(over_dz, x)


def last_kernel(
    counts_ref, send_ref, sent_leaves, sent_parents, turned_ref, self_hbm, leaf_ref,
    par_ref, in0, in1, in2, in3, out_ref, slab_ref, terms_ref, field_ref, near_sum, sem,
):
    incoming = (in0, in1, in2, in3)
    lane128 = iota((1, 128), 1)
    fetch = pltpu.make_async_copy(self_hbm.at[pl.ds(0, LEAVES)], near_sum, sem.at[0])
    fetch.start()
    leaf = leaf_ref[...]
    par = par_ref[...]
    for q in range(4):
        block = get_block(lambda s, q=q: incoming[q][SLOTS + s])
        ids = id_row(sent_leaves, sent_parents, q)
        leaf_hot = onehot_rows(LEAVES, jnp.where(lane128 < SLOTS, ids, -1))
        parent_hot = onehot_rows(128, jnp.where(lane128 >= SLOTS, ids, -1))
        leaf = leaf + pick(block, leaf_hot, True)
        par = par + pick(block, parent_hot, True)

    fetch.wait()
    for q in range(4):

        def arrive(step, _, q=q):
            first = step * 8
            places = [send_ref[0, q * SLOTS + first + k] for k in range(8)]
            values = [near_sum[c] + incoming[q][first + k] for k, c in enumerate(places)]
            for c, value in zip(places, values):
                near_sum[c] = value
            return 0

        lax.fori_loop(0, SLOTS // 8, arrive, 0)
    lane_parent = (iota((128, LEAVES), 1) // CZ % CY // 2) * (CZ // 2) + iota(
        (128, LEAVES), 1
    ) % CZ // 2
    above = pick(par, jnp.where(lane_parent == iota((128, LEAVES), 0), 1.0, 0.0).astype(bf16))
    terms = {alpha: above[n : n + 1, :] for n, alpha in enumerate(ALPHAS)}
    terms = shift_terms(terms, parent_offsets())
    for n, alpha in enumerate(ALPHAS):
        terms_ref[n : n + 1, :] = leaf[n : n + 1, :] + terms[alpha]

    for half in range(2):
        lanes = slice(half * 128, half * 128 + 128)

        def term(alpha):
            return terms_ref[AT[alpha] : AT[alpha] + 1, lanes]

        coefs = {alpha: term(alpha) * (1.0 / afact(alpha)) for alpha in ALPHAS}

        def chunk(step, _, coefs=coefs, lanes=lanes):
            rows = pl.ds(pl.multiple_of(step * 32, 32), 32)
            x, y, z = [turned_ref[comp, rows, lanes] for comp in range(1, 4)]
            value, *slopes = polynomial(lambda alpha: coefs[alpha], x, y, z)
            field_ref[0, rows, lanes] = value
            for comp, slope in enumerate(slopes):
                field_ref[comp + 1, rows, lanes] = -slope
            return 0

        lax.fori_loop(0, LEAF // 32, chunk, 0)

    for comp in range(4):
        turned = field_ref[comp].T
        for half in range(2):
            slab_ref[pl.ds(half * LEAVES * 8 + comp, LEAVES, stride=8), :] = turned[
                :, half * 128 : half * 128 + 128
            ]

    lane = iota((4, LEAF), 1)

    def write(c, _):
        value = jnp.concatenate(
            [
                slab_ref[pl.ds(pl.multiple_of(half * LEAVES * 8 + c * 8, 8), 8), :]
                for half in range(2)
            ],
            1,
        )[0:4] + near_sum[c]
        start = pl.multiple_of(c * LEAF, LEAF)
        out_ref[:, pl.ds(start, LEAF)] = jnp.where(lane < counts_ref[c], value, 0.0)
        return 0

    lax.fori_loop(0, LEAVES, write, 0, unroll=8)


def last(counts, send_leaves, send_parents, turned, near, leaf, par, arrived):
    return pl.pallas_call(
        last_kernel,
        name="last",
        out_shape=shaped(4, LEAVES * LEAF),
        in_specs=[SM, SM, VM, VM, VM, HB] + [VM] * 6,
        out_specs=VM,
        scratch_shapes=[
            pltpu.VMEM((LEAVES * 16, 128), f32),
            pltpu.VMEM((40, LEAVES), f32),
            pltpu.VMEM((4, LEAF, LEAVES), f32),
            pltpu.VMEM((LEAVES, 4, LEAF), f32),
            pltpu.SemaphoreType.DMA((1,)),
        ],
        compiler_params=pltpu.CompilerParams(**PARAMS),
    )(
        counts, send_leaves, send_leaves, send_parents, turned, near, leaf, par, *arrived
    )


def image_shift(slab_at, sub_at, slab_count, sub_count):
    rows_out = []
    for direction in range(4):
        reach_x = slab_at + slab_steps[direction]
        reach_y = sub_at + sub_steps[direction]
        jump_x = (reach_x - reach_x % slab_count) * CX
        jump_y = (reach_y - reach_y % sub_count) * CY
        rows_out.append(jnp.stack([jump_x, jump_y]))
    return jnp.stack(rows_out).astype(f32)


def moved_by(value, slab_step, sub_step, slab_count, sub_count):
    pairs = []
    for slab_at in range(slab_count):
        for sub_at in range(sub_count):
            target = (slab_at + slab_step) % slab_count * sub_count + (sub_at + sub_step) % sub_count
            pairs.append((slab_at * sub_count + sub_at, target))
    return lax.ppermute(value, ("slab", "sub"), pairs)


def on_device(
    positions, masses, leaf_counts, send_leaves, send_parents, near_pairs, far_pairs, parent_pairs
):
    slab_count = lax.axis_size("slab")
    sub_count = lax.axis_size("sub")
    slab_at = lax.axis_index("slab")
    sub_at = lax.axis_index("sub")
    at = jnp.stack([slab_at, sub_at]).astype(jnp.int32)
    own, cells, pcells, *outgoing, turned, leaf_order = front(
        at, leaf_counts, send_leaves, send_parents, positions, masses
    )
    incoming = [
        moved_by(outgoing[q], -slab_steps[q], -sub_steps[q], slab_count, sub_count)
        for q in range(4)
    ]
    image = image_shift(slab_at, sub_at, slab_count, sub_count)
    self0 = self_part(0, leaf_order, own)
    leaf, par, backs, ordered = far_part(
        image, far_pairs, parent_pairs, near_pairs, cells, pcells, incoming
    )
    near, *returning = near_part(ordered, own, incoming, backs, self0)
    arrived = [
        moved_by(returning[q], slab_steps[q], sub_steps[q], slab_count, sub_count)
        for q in range(4)
    ]
    near = self_part(1, leaf_order, own, near)
    return last(
        leaf_counts, send_leaves, send_parents, turned, near, leaf, par, arrived
    )


def solution(mesh):
    return jax.shard_map(
        on_device,
        mesh=mesh,
        in_specs=(
            P(None, ("slab", "sub")),
            P(("slab", "sub")),
            P(("slab", "sub")),
            P(("slab", "sub"), None),
            P(("slab", "sub"), None),
            P(("slab", "sub"), None, None),
            P(("slab", "sub"), None, None),
            P(("slab", "sub"), None, None),
        ),
        out_specs=P(None, ("slab", "sub")),
        check_vma=False,
    )
```

profile of v0, /device:TPU:1, one launch (start us, length us, event | category | flops | bytes accessed | tf_op | source)
XLA Modules:
  0.0 78.7 jit_solution(10451222533883794695)
XLA Ops:
  0.0 0.1 pad_add_fusion.at_ref
  0.1 6.5 %front.1 = (f32[256,4,256]{2,1,0:T(4,128)S(1)}, f32[40,256]{1,0:T(8,128)S(1)}, f32[40,128]{1,0:T(8,128)S(1)}, f32[69,4,256]{2,1,0:T(4,128)}, f32[69,4,256]{2,1,0...) custom-call(s32[2]{0:T(128)S(1)} %pad_add_fusion.at_ref, ...), custom_call_target="tpu_custom_call" | custom-call | tf_op jit(solution)/shard_map/front/pallas_call | solution.py:305
  6.6 1.4 %collective-permute-start = (f32[69,4,256]{2,1,0:T(4,128)}, f32[69,4,256]{2,1,0:T(4,128)S(1)}, u32[]{:S(2)}, u32[]{:S(2)}) collective-permute-start(f32[69,4,256]{2,1,0:T(4,128)} %get-tuple-element.28), channel_id=1, source_target_pairs={{0,112},{1,113},{2,114},{3,115},{4,116},{5,117},{6,118},{7,119},{8... | collective-permute-start | bytes 847880 | tf_op jit(solution)/shard_map/ppermute | solution.py:985
  8.1 6.0 %collective-permute-start.1 = (f32[69,4,256]{2,1,0:T(4,128)}, f32[69,4,256]{2,1,0:T(4,128)S(1)}, u32[]{:S(2)}, u32[]{:S(2)}) collective-permute-start(f32[69,4,256]{2,1,0:T(4,128)} %get-tuple-element.29), channel_id=1, source_target_pairs={{0,15},{1,0},{2,1},{3,2},{4,3},{5,4},{6,5},{7,6},{8,7},{9,8},{10,9... | collective-permute-start | bytes 847880 | tf_op jit(solution)/shard_map/ppermute | solution.py:985
  14.1 3.2 %collective-permute-start.2 = (f32[69,4,256]{2,1,0:T(4,128)}, f32[69,4,256]{2,1,0:T(4,128)S(1)}, u32[]{:S(2)}, u32[]{:S(2)}) collective-permute-start(f32[69,4,256]{2,1,0:T(4,128)} %get-tuple-element.30), channel_id=1, source_target_pairs={{0,127},{1,112},{2,113},{3,114},{4,115},{5,116},{6,117},{7,118},{8... | collective-permute-start | bytes 847880 | tf_op jit(solution)/shard_map/ppermute | solution.py:985
  17.3 1.0 %collective-permute-start.3 = (f32[69,4,256]{2,1,0:T(4,128)}, f32[69,4,256]{2,1,0:T(4,128)S(1)}, u32[]{:S(2)}, u32[]{:S(2)}) collective-permute-start(f32[69,4,256]{2,1,0:T(4,128)} %get-tuple-element.31), channel_id=1, source_target_pairs={{0,113},{1,114},{2,115},{3,116},{4,117},{5,118},{6,119},{7,120},{8... | collective-permute-start | bytes 847880 | tf_op jit(solution)/shard_map/ppermute | solution.py:985
  18.3 0.0 copy-start
  18.3 0.0 copy-start.3
  18.3 0.0 copy-start.5
  18.3 10.1 %self_part.2.self_ref = f32[264,8,256]{2,1,0:T(8,128)S(1)} custom-call(s32[2,384]{1,0:T(2,128)S(1)} %get-tuple-element.24.list_ref, f32[256,4,256]{2,1,0:T(4,128)S(1)} %get-tuple-element.25.own_ref), custom_call_target="tpu_custom_call" | custom-call | flops 5120000000 | bytes 2097152 | tf_op jit(solution)/shard_map/self_part/pallas_call | solution.py:469
  28.4 0.1 add_bitcast_fusion
  28.5 0.1 add_bitcast_fusion.1
  28.6 0.0 collective-permute-done.in0
  28.6 0.0 collective-permute-done.1.in1
  28.6 0.0 collective-permute-done.2.in2
  28.6 1.1 %collective-permute-done.3.in3 = f32[69,4,256]{2,1,0:T(4,128)S(1)} collective-permute-done((f32[69,4,256]{2,1,0:T(4,128)}, f32[69,4,256]{2,1,0:T(4,128)S(1)}, u32[]{:S(2)}, u32[]{:S(2)}) %collective-permute-start.3) | collective-permute-done | bytes 282656 | tf_op jit(solution)/shard_map/ppermute | solution.py:985
  29.8 0.0 copy-done
  29.8 0.0 copy-done.3
  29.8 0.0 copy-done.5
  29.8 3.3 %far_part.1 = (f32[40,256]{1,0:T(8,128)S(1)}, f32[40,128]{1,0:T(8,128)S(1)}, f32[4,40,128]{2,1,0:T(8,128)S(1)}, s32[2,384]{1,0:T(2,128)S(1)}) custom-call(f32[4,2]{1,0:T(4,128)S(1)} %add_convert_fusion.image_ref, s32[3,1,1024]{2,1,0:T(1,128)S(1)} %bitcast.20, s32[3,1,64]{2,1,0:T(1,128)S(1)} %bitcast.23, s32[3,1,256]{2,1,0:T(1,128)S(1)} %bitcast.22, ...), custom_call_target="tpu_custom_call" | custom-call | tf_op jit(solution)/shard_map/far_part/pallas_call | solution.py:797
  33.1 13.7 %near_part.1 = (f32[256,8,256]{2,1,0:T(8,128)S(1)}, f32[69,4,256]{2,1,0:T(4,128)S(1)}, f32[69,4,256]{2,1,0:T(4,128)S(1)}, f32[69,4,256]{2,1,0:T(4,128)S(1)}, f32[69,4,256]{2,1,0:T(4,128)S(1)}) custom-call(s32[2,384]{1,0:T(2,128)S(1)} %get-tuple-element.32.list_ref, f32[256,4,256]{2,1,0:T(4,128)S(1)} %get-tuple-element.25.own_ref, ...), custom_call_target="tpu_custom_call" | custom-call | flops 20480000000 | bytes 4000000 | tf_op jit(solution)/shard_map/near_part/pallas_call | solution.py:589
  46.7 8.0 %collective-permute-start.4 = (f32[69,4,256]{2,1,0:T(4,128)S(1)}, f32[69,4,256]{2,1,0:T(4,128)S(1)}, u32[]{:S(2)}, u32[]{:S(2)}) collective-permute-start(f32[69,4,256]{2,1,0:T(4,128)S(1)} %get-tuple-element.37), channel_id=1, source_target_pairs={{0,16},{1,17},{2,18},{3,19},{4,20},{5,21},{6,22},{7,23},{8,24},{9,... | collective-permute-start | bytes 847880 | tf_op jit(solution)/shard_map/ppermute | solution.py:985
  54.8 0.0 collective-permute-start.5
  54.8 0.0 collective-permute-start.6
  54.8 4.9 %collective-permute-start.7 = (f32[69,4,256]{2,1,0:T(4,128)S(1)}, f32[69,4,256]{2,1,0:T(4,128)S(1)}, u32[]{:S(2)}, u32[]{:S(2)}) collective-permute-start(f32[69,4,256]{2,1,0:T(4,128)S(1)} %get-tuple-element.40), channel_id=1, source_target_pairs={{0,31},{1,16},{2,17},{3,18},{4,19},{5,20},{6,21},{7,22},{8,23},{9,... | collective-permute-start | bytes 847880 | tf_op jit(solution)/shard_map/ppermute | solution.py:985
  59.6 0.0 copy-start.1
  59.6 0.0 copy-start.2
  59.6 0.0 copy-start.4
  59.6 11.7 %self_part.3.self_hbm = f32[264,4,256]{2,1,0:T(4,128)S(1)} custom-call(s32[2,384]{1,0:T(2,128)S(1)} %get-tuple-element.24.list_ref, f32[256,4,256]{2,1,0:T(4,128)S(1)} %get-tuple-element.25.own_ref, f32[256,8,256]{2,1,0:T(8,128)S(1)} %get-tuple-element.34.refs_0_), custom_call_target="tpu_custom_call" | custom-call | flops 5120000000 | bytes 2097152 | tf_op jit(solution)/shard_map/self_part/pallas_call | solution.py:469
  71.3 0.0 collective-permute-done.4.in0
  71.3 0.0 collective-permute-done.5.in1
  71.3 2.2 %collective-permute-done.6.in2 = f32[69,4,256]{2,1,0:T(4,128)S(1)} collective-permute-done((f32[69,4,256]{2,1,0:T(4,128)S(1)}, f32[69,4,256]{2,1,0:T(4,128)S(1)}, u32[]{:S(2)}, u32[]{:S(2)}) %collective-permute-start.6) | collective-permute-done | bytes 282656 | tf_op jit(solution)/shard_map/ppermute | solution.py:985
  73.5 0.0 collective-permute-done.7.in3
  73.5 0.0 copy-done.1
  73.6 0.0 copy-done.2
  73.6 0.0 copy-done.4
  73.6 5.0 %last.1 = f32[4,65536]{1,0:T(4,128)} custom-call(s32[256]{0:T(256)S(1)} %copy-done.1, s32[1,256]{1,0:T(1,128)S(1)} %copy-done.2, s32[1,256]{1,0:T(1,128)S(1)} %copy-done.2, s32[1,64]{1,0:T(1,128)S(1)} %copy-done.4, f32[4,256,256]{2,1,0:T(8,128)S(1)} %get-tuple-element.23.turned_ref, f32[264,4,256]{2,1,0:T(4,128)S(1)} %self_part.3.self_hbm, ...), custom_call_target="tpu_custom_call" | custom-call | tf_op jit(solution)/shard_map/last/pallas_call | solution.py:949
  (1 shorter events, 0.0 us)
Async XLA Ops:
  6.6 22.0 %collective-permute-start = (f32[69,4,256]{2,1,0:T(4,128)}, f32[69,4,256]{2,1,0:T(4,128)S(1)}, u32[]{:S(2)}, u32[]{:S(2)}) collective-permute-start(f32[69,4,256]{2,1,0:T(4,128)} %get-tuple-element.28), channel_id=1, source_target_pairs={{0,112},{1,113},{2,114},{3,115},{4,116},{5,117},{6,118},{7,119},{8... | collective-permute-start | bytes 847880 | tf_op jit(solution)/shard_map/ppermute | solution.py:985
  8.1 20.6 %collective-permute-start.1 = (f32[69,4,256]{2,1,0:T(4,128)}, f32[69,4,256]{2,1,0:T(4,128)S(1)}, u32[]{:S(2)}, u32[]{:S(2)}) collective-permute-start(f32[69,4,256]{2,1,0:T(4,128)} %get-tuple-element.29), channel_id=1, source_target_pairs={{0,15},{1,0},{2,1},{3,2},{4,3},{5,4},{6,5},{7,6},{8,7},{9,8},{10,9... | collective-permute-start | bytes 847880 | tf_op jit(solution)/shard_map/ppermute | solution.py:985
  14.1 14.5 %collective-permute-start.2 = (f32[69,4,256]{2,1,0:T(4,128)}, f32[69,4,256]{2,1,0:T(4,128)S(1)}, u32[]{:S(2)}, u32[]{:S(2)}) collective-permute-start(f32[69,4,256]{2,1,0:T(4,128)} %get-tuple-element.30), channel_id=1, source_target_pairs={{0,127},{1,112},{2,113},{3,114},{4,115},{5,116},{6,117},{7,118},{8... | collective-permute-start | bytes 847880 | tf_op jit(solution)/shard_map/ppermute | solution.py:985
  17.3 12.5 %collective-permute-start.3 = (f32[69,4,256]{2,1,0:T(4,128)}, f32[69,4,256]{2,1,0:T(4,128)S(1)}, u32[]{:S(2)}, u32[]{:S(2)}) collective-permute-start(f32[69,4,256]{2,1,0:T(4,128)} %get-tuple-element.31), channel_id=1, source_target_pairs={{0,113},{1,114},{2,115},{3,116},{4,117},{5,118},{6,119},{7,120},{8... | collective-permute-start | bytes 847880 | tf_op jit(solution)/shard_map/ppermute | solution.py:985
  18.3 11.5 %copy-start = (s32[1,3,1024]{2,0,1:T(1,128)S(1)}, s32[1,3,1024]{2,0,1:T(1,128)}, u32[]{:S(2)}) copy-start(s32[1,3,1024]{2,0,1:T(1,128)} %param.14) | copy-start | bytes 36868
  18.3 11.5 %copy-start.3 = (s32[1,3,256]{2,0,1:T(1,128)S(1)}, s32[1,3,256]{2,0,1:T(1,128)}, u32[]{:S(2)}) copy-start(s32[1,3,256]{2,0,1:T(1,128)} %param.13) | copy-start | bytes 9220
  18.3 11.5 %copy-start.5 = (s32[1,3,64]{2,0,1:T(1,128)S(1)}, s32[1,3,64]{2,0,1:T(1,128)}, u32[]{:S(2)}) copy-start(s32[1,3,64]{2,0,1:T(1,128)} %param.15) | copy-start | bytes 2308
  46.7 24.6 %collective-permute-start.4 = (f32[69,4,256]{2,1,0:T(4,128)S(1)}, f32[69,4,256]{2,1,0:T(4,128)S(1)}, u32[]{:S(2)}, u32[]{:S(2)}) collective-permute-start(f32[69,4,256]{2,1,0:T(4,128)S(1)} %get-tuple-element.37), channel_id=1, source_target_pairs={{0,16},{1,17},{2,18},{3,19},{4,20},{5,21},{6,22},{7,23},{8,24},{9,... | collective-permute-start | bytes 847880 | tf_op jit(solution)/shard_map/ppermute | solution.py:985
  54.8 16.6 %collective-permute-start.5 = (f32[69,4,256]{2,1,0:T(4,128)S(1)}, f32[69,4,256]{2,1,0:T(4,128)S(1)}, u32[]{:S(2)}, u32[]{:S(2)}) collective-permute-start(f32[69,4,256]{2,1,0:T(4,128)S(1)} %get-tuple-element.38), channel_id=1, source_target_pairs={{0,1},{1,2},{2,3},{3,4},{4,5},{5,6},{6,7},{7,8},{8,9},{9,10},{10,1... | collective-permute-start | bytes 847880 | tf_op jit(solution)/shard_map/ppermute | solution.py:985
  54.8 18.8 %collective-permute-start.6 = (f32[69,4,256]{2,1,0:T(4,128)S(1)}, f32[69,4,256]{2,1,0:T(4,128)S(1)}, u32[]{:S(2)}, u32[]{:S(2)}) collective-permute-start(f32[69,4,256]{2,1,0:T(4,128)S(1)} %get-tuple-element.39), channel_id=1, source_target_pairs={{0,17},{1,18},{2,19},{3,20},{4,21},{5,22},{6,23},{7,24},{8,25},{9,... | collective-permute-start | bytes 847880 | tf_op jit(solution)/shard_map/ppermute | solution.py:985
  54.8 18.8 %collective-permute-start.7 = (f32[69,4,256]{2,1,0:T(4,128)S(1)}, f32[69,4,256]{2,1,0:T(4,128)S(1)}, u32[]{:S(2)}, u32[]{:S(2)}) collective-permute-start(f32[69,4,256]{2,1,0:T(4,128)S(1)} %get-tuple-element.40), channel_id=1, source_target_pairs={{0,31},{1,16},{2,17},{3,18},{4,19},{5,20},{6,21},{7,22},{8,23},{9,... | collective-permute-start | bytes 847880 | tf_op jit(solution)/shard_map/ppermute | solution.py:985
  59.6 13.9 %copy-start.1 = (s32[256]{0:T(256)S(1)}, s32[256]{0:T(256)}, u32[]{:S(2)}) copy-start(s32[256]{0:T(256)} %counts_ref.1) | copy-start | bytes 3076
  59.6 13.9 %copy-start.2 = (s32[1,256]{1,0:T(1,128)S(1)}, s32[1,256]{1,0:T(1,128)}, u32[]{:S(2)}) copy-start(s32[1,256]{1,0:T(1,128)} %sent_leaves.1) | copy-start | bytes 3076
  59.6 13.9 %copy-start.4 = (s32[1,64]{1,0:T(1,128)S(1)}, s32[1,64]{1,0:T(1,128)}, u32[]{:S(2)}) copy-start(s32[1,64]{1,0:T(1,128)} %sent_parents.1) | copy-start | bytes 772
where the time goes:
time: 77.9 us; the launch traced here: 78.7 us
  Pallas kernels  50.2 us (64%)
  starting transfers between devices  24.6 us (32%)
  waiting for transfers between devices  3.37 us (4%)
    ppermute x8, starting transfers between devices, moved_by(): return lax.ppermute(value, ('slab', 'sub'), pairs)  24.6 us
    pallas_call x2, Pallas kernels, self_part(): pl.pallas_call(functools.partial(self_kernel, part), name='self_part', ou...  21.8 us
    pallas_call x1, Pallas kernels, near_part(): pl.pallas_call(near_kernel, name='near_part', out_shape=[shaped(LEAVES, 8...  13.7 us
    pallas_call x1, Pallas kernels, front(): pl.pallas_call(front_kernel, name='front', out_shape=[shaped(LEAVES, 4, L...  6.54 us
    pallas_call x1, Pallas kernels, last(): pl.pallas_call(last_kernel, name='last', out_shape=shaped(4, LEAVES * LEA...  4.98 us
    ppermute x8, waiting for transfers between devices, moved_by(): return lax.ppermute(value, ('slab', 'sub'), pairs)  3.37 us
    pallas_call x1, Pallas kernels, far_part(): pl.pallas_call(far_kernel, name='far_part', out_shape=[shaped(40, LEAVES)...  3.27 us
  transfers between devices with their start and end apart: 8, of which 2 were waited for; matrix products, arithmetic and copies ran while one was open for 0% of the time, Pallas kernels for 28%

commit v1 on v0

--- a/solution.py
+++ b/solution.py
@@ -448,7 +448,7 @@
     for n, rows in enumerate(CLASSES):
         first = list_ref[1, n]
         end = list_ref[1, n + 1]
-        middle = (first + end + n % 2) >> 1
+        middle = jnp.minimum((first + end + n) >> 1, end)
         lanes = 128 if rows == 128 else LEAF
 
         def body(step, _, rows=rows, lanes=lanes):

time: 77.9 us -> 77.3 us (level); the launches traced: 78.7 us -> 77.2 us
  waiting for transfers between devices: 3.37 us -> 0.54 us
  starting transfers between devices: 24.6 us -> 26.7 us
  Pallas kernels: 50.2 us -> 49.4 us
    ppermute x8, waiting for transfers between devices: 3.37 us -> 0.54 us  [moved_by(): return lax.ppermute(value, ('slab', 'sub'), pairs)]
    ppermute x8, starting transfers between devices: 24.6 us -> 26.7 us  [moved_by(): return lax.ppermute(value, ('slab', 'sub'), pairs)]
    pallas_call x2, Pallas kernels: 21.8 us -> 21 us  [self_part(): pl.pallas_call(functools.partial(self_kernel, part), name='self_part', ou...]
  transfers between devices with their start and end apart: 8 -> 8, of which waited for: 2 -> 1; matrix products, arithmetic and copies ran while one was open for 0% -> 0% of each run, Pallas kernels for 28% -> 27%
where the time goes in v1:
time: 77.3 us; the launch traced here: 77.2 us
  Pallas kernels  49.4 us (64%)
  starting transfers between devices  26.7 us (35%)
    ppermute x8, starting transfers between devices, moved_by(): return lax.ppermute(value, ('slab', 'sub'), pairs)  26.7 us
    pallas_call x2, Pallas kernels, self_part(): pl.pallas_call(functools.partial(self_kernel, part), name='self_part', ou...  21 us
    pallas_call x1, Pallas kernels, near_part(): pl.pallas_call(near_kernel, name='near_part', out_shape=[shaped(LEAVES, 8...  13.6 us
    pallas_call x1, Pallas kernels, front(): pl.pallas_call(front_kernel, name='front', out_shape=[shaped(LEAVES, 4, L...  6.54 us
    pallas_call x1, Pallas kernels, last(): pl.pallas_call(last_kernel, name='last', out_shape=shaped(4, LEAVES * LEA...  4.98 us
    pallas_call x1, Pallas kernels, far_part(): pl.pallas_call(far_kernel, name='far_part', out_shape=[shaped(40, LEAVES)...  3.27 us
  transfers between devices with their start and end apart: 8, of which 1 were waited for; matrix products, arithmetic and copies ran while one was open for 0% of the time, Pallas kernels for 27%

profile of v1, /device:TPU:1, one launch (start us, length us, event | category | flops | bytes accessed | tf_op | source)
XLA Modules:
  0.0 77.2 jit_solution(9561090991729674723)
XLA Ops:
  0.0 0.1 pad_add_fusion.at_ref
  0.1 6.5 %front.1 = (f32[256,4,256]{2,1,0:T(4,128)S(1)}, f32[40,256]{1,0:T(8,128)S(1)}, f32[40,128]{1,0:T(8,128)S(1)}, f32[69,4,256]{2,1,0:T(4,128)}, f32[69,4,256]{2,1,0...) custom-call(s32[2]{0:T(128)S(1)} %pad_add_fusion.at_ref, ...), custom_call_target="tpu_custom_call" | custom-call | tf_op jit(solution)/shard_map/front/pallas_call | solution.py:305
  6.6 1.4 %collective-permute-start = (f32[69,4,256]{2,1,0:T(4,128)}, f32[69,4,256]{2,1,0:T(4,128)S(1)}, u32[]{:S(2)}, u32[]{:S(2)}) collective-permute-start(f32[69,4,256]{2,1,0:T(4,128)} %get-tuple-element.28), channel_id=1, source_target_pairs={{0,112},{1,113},{2,114},{3,115},{4,116},{5,117},{6,118},{7,119},{8... | collective-permute-start | bytes 847880 | tf_op jit(solution)/shard_map/ppermute | solution.py:985
  8.1 6.0 %collective-permute-start.1 = (f32[69,4,256]{2,1,0:T(4,128)}, f32[69,4,256]{2,1,0:T(4,128)S(1)}, u32[]{:S(2)}, u32[]{:S(2)}) collective-permute-start(f32[69,4,256]{2,1,0:T(4,128)} %get-tuple-element.29), channel_id=1, source_target_pairs={{0,15},{1,0},{2,1},{3,2},{4,3},{5,4},{6,5},{7,6},{8,7},{9,8},{10,9... | collective-permute-start | bytes 847880 | tf_op jit(solution)/shard_map/ppermute | solution.py:985
  14.1 3.2 %collective-permute-start.2 = (f32[69,4,256]{2,1,0:T(4,128)}, f32[69,4,256]{2,1,0:T(4,128)S(1)}, u32[]{:S(2)}, u32[]{:S(2)}) collective-permute-start(f32[69,4,256]{2,1,0:T(4,128)} %get-tuple-element.30), channel_id=1, source_target_pairs={{0,127},{1,112},{2,113},{3,114},{4,115},{5,116},{6,117},{7,118},{8... | collective-permute-start | bytes 847880 | tf_op jit(solution)/shard_map/ppermute | solution.py:985
  17.3 1.0 %collective-permute-start.3 = (f32[69,4,256]{2,1,0:T(4,128)}, f32[69,4,256]{2,1,0:T(4,128)S(1)}, u32[]{:S(2)}, u32[]{:S(2)}) collective-permute-start(f32[69,4,256]{2,1,0:T(4,128)} %get-tuple-element.31), channel_id=1, source_target_pairs={{0,113},{1,114},{2,115},{3,116},{4,117},{5,118},{6,119},{7,120},{8... | collective-permute-start | bytes 847880 | tf_op jit(solution)/shard_map/ppermute | solution.py:985
  18.3 0.0 copy-start
  18.3 0.0 copy-start.3
  18.3 0.0 copy-start.5
  18.3 10.7 %self_part.2.self_ref = f32[264,8,256]{2,1,0:T(8,128)S(1)} custom-call(s32[2,384]{1,0:T(2,128)S(1)} %get-tuple-element.24.list_ref, f32[256,4,256]{2,1,0:T(4,128)S(1)} %get-tuple-element.25.own_ref), custom_call_target="tpu_custom_call" | custom-call | flops 5120000000 | bytes 2097152 | tf_op jit(solution)/shard_map/self_part/pallas_call | solution.py:469
  29.1 0.1 add_bitcast_fusion
  29.1 0.1 add_bitcast_fusion.1
  29.2 0.0 collective-permute-done.in0
  29.2 0.0 collective-permute-done.1.in1
  29.2 0.0 collective-permute-done.2.in2
  29.3 0.5 collective-permute-done.3.in3
  29.8 0.0 copy-done
  29.8 0.0 copy-done.3
  29.8 0.0 copy-done.5
  29.8 3.3 %far_part.1 = (f32[40,256]{1,0:T(8,128)S(1)}, f32[40,128]{1,0:T(8,128)S(1)}, f32[4,40,128]{2,1,0:T(8,128)S(1)}, s32[2,384]{1,0:T(2,128)S(1)}) custom-call(f32[4,2]{1,0:T(4,128)S(1)} %add_convert_fusion.image_ref, s32[3,1,1024]{2,1,0:T(1,128)S(1)} %bitcast.20, s32[3,1,64]{2,1,0:T(1,128)S(1)} %bitcast.23, s32[3,1,256]{2,1,0:T(1,128)S(1)} %bitcast.22, ...), custom_call_target="tpu_custom_call" | custom-call | tf_op jit(solution)/shard_map/far_part/pallas_call | solution.py:797
  33.1 13.6 %near_part.1 = (f32[256,8,256]{2,1,0:T(8,128)S(1)}, f32[69,4,256]{2,1,0:T(4,128)S(1)}, f32[69,4,256]{2,1,0:T(4,128)S(1)}, f32[69,4,256]{2,1,0:T(4,128)S(1)}, f32[69,4,256]{2,1,0:T(4,128)S(1)}) custom-call(s32[2,384]{1,0:T(2,128)S(1)} %get-tuple-element.32.list_ref, f32[256,4,256]{2,1,0:T(4,128)S(1)} %get-tuple-element.25.own_ref, ...), custom_call_target="tpu_custom_call" | custom-call | flops 20480000000 | bytes 4000000 | tf_op jit(solution)/shard_map/near_part/pallas_call | solution.py:589
  46.7 10.1 %collective-permute-start.4 = (f32[69,4,256]{2,1,0:T(4,128)S(1)}, f32[69,4,256]{2,1,0:T(4,128)S(1)}, u32[]{:S(2)}, u32[]{:S(2)}) collective-permute-start(f32[69,4,256]{2,1,0:T(4,128)S(1)} %get-tuple-element.37), channel_id=1, source_target_pairs={{0,16},{1,17},{2,18},{3,19},{4,20},{5,21},{6,22},{7,23},{8,24},{9,... | collective-permute-start | bytes 847880 | tf_op jit(solution)/shard_map/ppermute | solution.py:985
  56.9 0.0 collective-permute-start.5
  56.9 0.0 collective-permute-start.6
  56.9 4.9 %collective-permute-start.7 = (f32[69,4,256]{2,1,0:T(4,128)S(1)}, f32[69,4,256]{2,1,0:T(4,128)S(1)}, u32[]{:S(2)}, u32[]{:S(2)}) collective-permute-start(f32[69,4,256]{2,1,0:T(4,128)S(1)} %get-tuple-element.40), channel_id=1, source_target_pairs={{0,31},{1,16},{2,17},{3,18},{4,19},{5,20},{6,21},{7,22},{8,23},{9,... | collective-permute-start | bytes 847880 | tf_op jit(solution)/shard_map/ppermute | solution.py:985
  61.7 0.0 copy-start.1
  61.7 0.0 copy-start.2
  61.7 0.0 copy-start.4
  61.7 10.2 %self_part.3.self_hbm = f32[264,4,256]{2,1,0:T(4,128)S(1)} custom-call(s32[2,384]{1,0:T(2,128)S(1)} %get-tuple-element.24.list_ref, f32[256,4,256]{2,1,0:T(4,128)S(1)} %get-tuple-element.25.own_ref, f32[256,8,256]{2,1,0:T(8,128)S(1)} %get-tuple-element.34.refs_0_), custom_call_target="tpu_custom_call" | custom-call | flops 5120000000 | bytes 2097152 | tf_op jit(solution)/shard_map/self_part/pallas_call | solution.py:469
  71.9 0.0 collective-permute-done.4.in0
  72.0 0.0 collective-permute-done.5.in1
  72.0 0.0 collective-permute-done.6.in2
  72.0 0.0 collective-permute-done.7.in3
  72.0 0.0 copy-done.1
  72.0 0.0 copy-done.2
  72.0 0.0 copy-done.4
  72.0 5.0 %last.1 = f32[4,65536]{1,0:T(4,128)} custom-call(s32[256]{0:T(256)S(1)} %copy-done.1, s32[1,256]{1,0:T(1,128)S(1)} %copy-done.2, s32[1,256]{1,0:T(1,128)S(1)} %copy-done.2, s32[1,64]{1,0:T(1,128)S(1)} %copy-done.4, f32[4,256,256]{2,1,0:T(8,128)S(1)} %get-tuple-element.23.turned_ref, f32[264,4,256]{2,1,0:T(4,128)S(1)} %self_part.3.self_hbm, ...), custom_call_target="tpu_custom_call" | custom-call | tf_op jit(solution)/shard_map/last/pallas_call | solution.py:949
  (1 shorter events, 0.0 us)
Async XLA Ops:
  6.6 22.6 %collective-permute-start = (f32[69,4,256]{2,1,0:T(4,128)}, f32[69,4,256]{2,1,0:T(4,128)S(1)}, u32[]{:S(2)}, u32[]{:S(2)}) collective-permute-start(f32[69,4,256]{2,1,0:T(4,128)} %get-tuple-element.28), channel_id=1, source_target_pairs={{0,112},{1,113},{2,114},{3,115},{4,116},{5,117},{6,118},{7,119},{8... | collective-permute-start | bytes 847880 | tf_op jit(solution)/shard_map/ppermute | solution.py:985
  8.1 21.2 %collective-permute-start.1 = (f32[69,4,256]{2,1,0:T(4,128)}, f32[69,4,256]{2,1,0:T(4,128)S(1)}, u32[]{:S(2)}, u32[]{:S(2)}) collective-permute-start(f32[69,4,256]{2,1,0:T(4,128)} %get-tuple-element.29), channel_id=1, source_target_pairs={{0,15},{1,0},{2,1},{3,2},{4,3},{5,4},{6,5},{7,6},{8,7},{9,8},{10,9... | collective-permute-start | bytes 847880 | tf_op jit(solution)/shard_map/ppermute | solution.py:985
  14.1 15.2 %collective-permute-start.2 = (f32[69,4,256]{2,1,0:T(4,128)}, f32[69,4,256]{2,1,0:T(4,128)S(1)}, u32[]{:S(2)}, u32[]{:S(2)}) collective-permute-start(f32[69,4,256]{2,1,0:T(4,128)} %get-tuple-element.30), channel_id=1, source_target_pairs={{0,127},{1,112},{2,113},{3,114},{4,115},{5,116},{6,117},{7,118},{8... | collective-permute-start | bytes 847880 | tf_op jit(solution)/shard_map/ppermute | solution.py:985
  17.3 12.5 %collective-permute-start.3 = (f32[69,4,256]{2,1,0:T(4,128)}, f32[69,4,256]{2,1,0:T(4,128)S(1)}, u32[]{:S(2)}, u32[]{:S(2)}) collective-permute-start(f32[69,4,256]{2,1,0:T(4,128)} %get-tuple-element.31), channel_id=1, source_target_pairs={{0,113},{1,114},{2,115},{3,116},{4,117},{5,118},{6,119},{7,120},{8... | collective-permute-start | bytes 847880 | tf_op jit(solution)/shard_map/ppermute | solution.py:985
  18.3 11.5 %copy-start = (s32[1,3,1024]{2,0,1:T(1,128)S(1)}, s32[1,3,1024]{2,0,1:T(1,128)}, u32[]{:S(2)}) copy-start(s32[1,3,1024]{2,0,1:T(1,128)} %param.14) | copy-start | bytes 36868
  18.3 11.5 %copy-start.3 = (s32[1,3,256]{2,0,1:T(1,128)S(1)}, s32[1,3,256]{2,0,1:T(1,128)}, u32[]{:S(2)}) copy-start(s32[1,3,256]{2,0,1:T(1,128)} %param.13) | copy-start | bytes 9220
  18.3 11.5 %copy-start.5 = (s32[1,3,64]{2,0,1:T(1,128)S(1)}, s32[1,3,64]{2,0,1:T(1,128)}, u32[]{:S(2)}) copy-start(s32[1,3,64]{2,0,1:T(1,128)} %param.15) | copy-start | bytes 2308
  46.7 25.2 %collective-permute-start.4 = (f32[69,4,256]{2,1,0:T(4,128)S(1)}, f32[69,4,256]{2,1,0:T(4,128)S(1)}, u32[]{:S(2)}, u32[]{:S(2)}) collective-permute-start(f32[69,4,256]{2,1,0:T(4,128)S(1)} %get-tuple-element.37), channel_id=1, source_target_pairs={{0,16},{1,17},{2,18},{3,19},{4,20},{5,21},{6,22},{7,23},{8,24},{9,... | collective-permute-start | bytes 847880 | tf_op jit(solution)/shard_map/ppermute | solution.py:985
  56.9 15.1 %collective-permute-start.5 = (f32[69,4,256]{2,1,0:T(4,128)S(1)}, f32[69,4,256]{2,1,0:T(4,128)S(1)}, u32[]{:S(2)}, u32[]{:S(2)}) collective-permute-start(f32[69,4,256]{2,1,0:T(4,128)S(1)} %get-tuple-element.38), channel_id=1, source_target_pairs={{0,1},{1,2},{2,3},{3,4},{4,5},{5,6},{6,7},{7,8},{8,9},{9,10},{10,1... | collective-permute-start | bytes 847880 | tf_op jit(solution)/shard_map/ppermute | solution.py:985
  56.9 15.1 %collective-permute-start.6 = (f32[69,4,256]{2,1,0:T(4,128)S(1)}, f32[69,4,256]{2,1,0:T(4,128)S(1)}, u32[]{:S(2)}, u32[]{:S(2)}) collective-permute-start(f32[69,4,256]{2,1,0:T(4,128)S(1)} %get-tuple-element.39), channel_id=1, source_target_pairs={{0,17},{1,18},{2,19},{3,20},{4,21},{5,22},{6,23},{7,24},{8,25},{9,... | collective-permute-start | bytes 847880 | tf_op jit(solution)/shard_map/ppermute | solution.py:985
  56.9 15.1 %collective-permute-start.7 = (f32[69,4,256]{2,1,0:T(4,128)S(1)}, f32[69,4,256]{2,1,0:T(4,128)S(1)}, u32[]{:S(2)}, u32[]{:S(2)}) collective-permute-start(f32[69,4,256]{2,1,0:T(4,128)S(1)} %get-tuple-element.40), channel_id=1, source_target_pairs={{0,31},{1,16},{2,17},{3,18},{4,19},{5,20},{6,21},{7,22},{8,23},{9,... | collective-permute-start | bytes 847880 | tf_op jit(solution)/shard_map/ppermute | solution.py:985
  61.7 10.3 %copy-start.1 = (s32[256]{0:T(256)S(1)}, s32[256]{0:T(256)}, u32[]{:S(2)}) copy-start(s32[256]{0:T(256)} %counts_ref.1) | copy-start | bytes 3076
  61.7 10.3 %copy-start.2 = (s32[1,256]{1,0:T(1,128)S(1)}, s32[1,256]{1,0:T(1,128)}, u32[]{:S(2)}) copy-start(s32[1,256]{1,0:T(1,128)} %sent_leaves.1) | copy-start | bytes 3076
  61.7 10.3 %copy-start.4 = (s32[1,64]{1,0:T(1,128)S(1)}, s32[1,64]{1,0:T(1,128)}, u32[]{:S(2)}) copy-start(s32[1,64]{1,0:T(1,128)} %sent_parents.1) | copy-start | bytes 772
